TPU v7x, 32 devices: a whole 2x2x4 slice. The times are simulated.
32 devices in a mesh: item: 2 (over core), site: 16 (over z, y, x).
Axes of the slice: x: 2, y: 2, z: 4, core: 2. Of those that a mesh axis runs over, the one named last changes fastest.
Arguments:
- item_factors: float32 [16, 32, 65536], P('site', None, 'item'), may hold values from -3 to 3
- user_factors: float32 [16, 32, 4096], P('site', None, 'item'), may hold values from -3 to 3
- ratings: bfloat16 [16, 2, 128, 128, 128], P('site', 'item'), may hold values from -6 to 6
- block_rows: int32 [16, 2, 128], P('site', 'item'), may hold values from 0 to 255, as said below
- block_cols: int32 [16, 2, 128], P('site', 'item'), may hold values from 0 to 31
- block_count: int32 [16, 2], P('site', 'item'), may hold values from 16 to 128, as said below
- hop_steps: int32 [2], replicated, may hold values from 0 to 2, as said below
Outputs:
- items_out: float32 [16, 32, 65536], P('site', None, 'item')
- users_out: float32 [16, 32, 4096], P('site', None, 'item')
Inputs may be any that keep to these rules, and one draw needn't show every extreme that they name: `block_rows`: within one device the live and empty slots name distinct pairs of blocks. `block_count`: some device has all 128 slots live. `hop_steps`: the steps' exponents differ.
All inputs are finite; a program needn't handle non-finite values.
Results may differ from a plain program's by a relative error of at most 0.0003.
Values sent between devices are 32-bit elements; how exact they have to be, the bound alone decides.
A program may use at most 128 MiB of HBM per device.

v0:
```python
from functools import partial

import jax
import jax.numpy as jnp
from jax import lax
from jax.experimental import pallas as pl
from jax.experimental.pallas import tpu as pltpu
from jax.sharding import PartitionSpec as P

ITERS = 2
HOPS = 3
LEARN_RATE = 0.05
CHUNKS = 4
GROUP = 8


def passed_along(block, axis, distance):
    devices = range(lax.axis_size(axis))
    route = [((i - distance) % len(devices), i) for i in devices]
    return lax.ppermute(block, axis, route)


def split_high_low(values):
    high = values.astype(jnp.bfloat16)
    low = (values - high.astype(jnp.float32)).astype(jnp.bfloat16)
    return high, low


def dot_f32(lhs, rhs, lhs_dim, rhs_dim):
    return lax.dot_general(
        lhs, rhs, (((lhs_dim,), (rhs_dim,)), ((), ())), preferred_element_type=jnp.float32
    )


def grads_kernel(chunks, rows_ref, cols_ref, count_ref, *refs):
    x_refs = refs[:chunks]
    y_ref, ratings_ref = refs[chunks : chunks + 2]
    base_refs = refs[chunks + 2 : 2 * chunks + 2]
    user_ref = refs[2 * chunks + 2]
    group, tile = ratings_ref.shape[0], ratings_ref.shape[-1]
    rank = y_ref.shape[0]
    part_rank = rank // chunks
    first = pl.program_id(0) * group
    total = count_ref[0]

    @pl.when(pl.program_id(0) == 0)
    def _():
        for x_ref, base_ref in zip(x_refs, base_refs):
            base_ref[...] = 0.5 * x_ref[...]
        user_ref[...] = jnp.zeros_like(user_ref)

    @pl.when(first < total)
    def _():
        parts = []
        for k in range(group):
            row = pl.ds(pl.multiple_of(rows_ref[first + k] * tile, tile), tile)
            col = pl.ds(pl.multiple_of(cols_ref[first + k] * tile, tile), tile)
            limit = jnp.where(first + k < total, 1.0, 0.0).astype(jnp.float32)
            x = jnp.concatenate([x_ref[:, row] for x_ref in x_refs], axis=0)
            x_high, x_low = split_high_low(x)
            y_high, y_low = split_high_low(y_ref[:, col])
            rebuilt = dot_f32(
                jnp.concatenate([x_high, x_low, x_high], axis=0),
                jnp.concatenate([y_high, y_high, y_low], axis=0),
                0,
                0,
            )
            clipped = jnp.clip(rebuilt - ratings_ref[k].astype(jnp.float32), -limit, limit)
            c_high, c_low = split_high_low(clipped)
            item_pair = dot_f32(jnp.concatenate([y_high, y_low], axis=0), c_high, 1, 1)
            item_part = item_pair[:rank] + item_pair[rank:] + dot_f32(y_high, c_low, 1, 1)
            user_pair = dot_f32(jnp.concatenate([x_high, x_low], axis=0), c_high, 1, 0)
            user_part = user_pair[:rank] + user_pair[rank:] + dot_f32(x_high, c_low, 1, 0)
            parts.append((row, col, item_part, user_part))
        for row, col, item_part, user_part in parts:
            for c, base_ref in enumerate(base_refs):
                base_ref[:, row] -= LEARN_RATE * item_part[c * part_rank : (c + 1) * part_rank]
            user_ref[:, col] += user_part


def local_grads(x_parts, users_whole, slot_values, row_index, column_index, block_total):
    chunks = len(x_parts)
    slot_total, tile = slot_values.shape[0], slot_values.shape[-1]
    rank, users = users_whole.shape
    items = x_parts[0].shape[1]
    once = pl.Buffered(1)
    x_spec = pl.BlockSpec(x_parts[0].shape, lambda i, *_: (0, 0), pipeline_mode=once)
    y_spec = pl.BlockSpec((rank, users), lambda i, *_: (0, 0), pipeline_mode=once)
    outs = pl.pallas_call(
        partial(grads_kernel, chunks),
        grid_spec=pltpu.PrefetchScalarGridSpec(
            num_scalar_prefetch=3,
            grid=(slot_total // GROUP,),
            in_specs=[x_spec] * chunks
            + [y_spec, pl.BlockSpec((GROUP, tile, tile), lambda i, *_: (i, 0, 0))],
            out_specs=[x_spec] * chunks + [y_spec],
        ),
        out_shape=[jax.ShapeDtypeStruct(p.shape, jnp.float32) for p in x_parts]
        + [jax.ShapeDtypeStruct((rank, users), jnp.float32)],
        compiler_params=pltpu.CompilerParams(vmem_limit_bytes=24 << 20),
        cost_estimate=pl.CostEstimate(
            flops=18 * slot_total * tile * tile * rank,
            bytes_accessed=8 * rank * items + 2 * slot_total * tile * tile,
            transcendentals=0,
        ),
    )(row_index, column_index, block_total, *x_parts, users_whole, slot_values)
    return outs[:chunks], outs[chunks]


def two_steps(hops, item_here, user_here, slot_values, row_index, column_index, block_total):
    rank = item_here.shape[0]
    size = rank // CHUNKS
    x_parts = [item_here[c * size : (c + 1) * size] for c in range(CHUNKS)]
    for hop in hops:
        peers = [passed_along(part, "site", -(1 << hop)) for part in x_parts]
        users_whole = lax.all_gather(user_here, "item", axis=1, tiled=True)
        bases, user_grad = local_grads(
            x_parts, users_whole, slot_values, row_index, column_index, block_total
        )
        x_parts = [base + 0.5 * peer for base, peer in zip(bases, peers)]
        owned = lax.psum_scatter(user_grad, "item", scatter_dimension=1, tiled=True)
        user_here = user_here - LEARN_RATE * owned
    return jnp.concatenate(x_parts, axis=0), user_here


def per_device(item_factors, user_factors, ratings, block_rows, block_cols, block_count, hop_steps):
    pairs = [(a, b) for a in range(HOPS) for b in range(HOPS) if a != b]
    first, second = hop_steps[0], hop_steps[1]
    chosen = first * (HOPS - 1) + second - (second > first).astype(jnp.int32)
    item_here, user_here = lax.switch(
        chosen,
        [partial(two_steps, pair) for pair in pairs],
        item_factors[0],
        user_factors[0],
        ratings[0, 0],
        block_rows[0, 0],
        block_cols[0, 0],
        block_count[0],
    )
    return (item_here[None], user_here[None])


def solution(mesh):
    return jax.shard_map(
        per_device,
        mesh=mesh,
        in_specs=(
            P("site", None, "item"),
            P("site", None, "item"),
            P("site", "item", None, None, None),
            P("site", "item", None),
            P("site", "item", None),
            P("site", "item"),
            P(),
        ),
        out_specs=(P("site", None, "item"), P("site", None, "item")),
        check_vma=False,
    )
```

profile of v0, /device:TPU:0, one launch (start us, length us, event | category | flops | bytes accessed | tf_op | source)
XLA Modules:
  0.0 212.0 jit_solution(18366248642908106732)
XLA Ops:
  7.2 1.3 fusion.6
  11.1 194.1 %conditional.1 = (f32[1,32,32768]{2,1,0:T(8,128)}, f32[1,32,2048]{2,1,0:T(8,128)}) conditional(s32[]{:T(128)} %clamp.3, (f32[32,32768]{1,0:T(8,128)}, f32[32,2048]{1,0:T(8,128)}, s32[128]{0:T(128)}, s32[128]{0:T(128)}, s32[1]{0:T(128)}, /*index=5*/bf16[128,128,128]{2,1,0:T(8,128)(2,1)}) %tuple.129, ...), branch_computations={%region_0.0_spmd, %region_3.0_spmd, %region_6.0_spmd, %region_9.0_... | conditional | flops 2423521280 | bytes 182981600 | solution.py:130
  11.4 3.6 %fusion.4 = (f32[8,32768]{1,0:T(8,128)}, f32[8,32768]{1,0:T(8,128)S(1)}, f32[8,32768]{1,0:T(8,128)S(1)}, f32[8,32768]{1,0:T(8,128)S(1)}) fusion(f32[32,32768]{1,0:T(8,128)} %get-tuple-element.141), kind=kLoop, calls=%fused_computation.70 | loop fusion | bytes 8388608 | tf_op jit(solution)/shard_map/cond/branch_4_fun/slice | solution.py:113
  15.0 5.0 %collective-permute-start.32 = (f32[8,32768]{1,0:T(8,128)S(1)}, f32[8,32768]{1,0:T(8,128)}, u32[]{:S(2)}, u32[]{:S(2)}) collective-permute-start(f32[8,32768]{1,0:T(8,128)S(1)} %get-tuple-element.193.refs_0_), channel_id=1, source_target_pairs={{4,0},{5,1},{6,2},{7,3},{8,4},{9,5},{10,6},{11,7},{12,8},{13,9},{1... | collective-permute-start | bytes 3145736 | tf_op jit(solution)/shard_map/cond/branch_4_fun/ppermute | solution.py:20
  21.0 2.2 %all_gather.32.refs_4_ = f32[32,4096]{1,0:T(8,128)S(1)} all-gather(f32[32,2048]{1,0:T(8,128)S(1)} %copy-done.94), channel_id=1, replica_groups=mesh['item'=2,'site'=16] {'item'}, dimensions={1}, use_global_device_ids=true | all-gather | bytes 786432 | tf_op jit(solution)/shard_map/cond/branch_4_fun/all_gather | solution.py:116
  23.2 15.0 %branch_4_fun.2 = (f32[8,32768]{1,0:T(8,128)S(1)}, f32[8,32768]{1,0:T(8,128)S(1)}, f32[8,32768]{1,0:T(8,128)S(1)}, f32[8,32768]{1,0:T(8,128)S(1)}, f32[32,4096]{1,0:T(8,128)S(1)}) custom-call(s32[128]{0:T(128)S(1)} %copy-done.112, s32[128]{0:T(128)S(1)} %copy-done.118, s32[1]{0:T(128)} %get-tuple-element.140.count_ref, ...), custom_call_target="tpu_custom_call" | custom-call | flops 1207959552 | bytes 12582912 | tf_op jit(solution)/shard_map/cond/branch_4_fun/pallas_call | solution.py:89
  38.2 1.0 copy-done.8
  39.1 1.0 copy-done.20
  41.2 1.0 copy-done.64
  43.6 1.7 multiply_add_fusion.39.refs_0_
  45.3 6.3 %collective-permute-start.36 = (f32[8,32768]{1,0:T(8,128)S(1)}, f32[8,32768]{1,0:T(8,128)}, u32[]{:S(2)}, u32[]{:S(2)}) collective-permute-start(f32[8,32768]{1,0:T(8,128)S(1)} %multiply_add_fusion.39.refs_0_), channel_id=1, source_target_pairs={{1,0},{2,1},{3,2},{4,3},{5,4},{6,5},{7,6},{8,7},{9,8},{10,9},{11,1... | collective-permute-start | bytes 3145736 | tf_op jit(solution)/shard_map/cond/branch_4_fun/ppermute | solution.py:20
  51.7 59.4 %collective-permute-done.33 = f32[8,32768]{1,0:T(8,128)} collective-permute-done((f32[8,32768]{1,0:T(8,128)S(1)}, f32[8,32768]{1,0:T(8,128)}, u32[]{:S(2)}, u32[]{:S(2)}) %collective-permute-start.33) | collective-permute-done | bytes 1048608 | tf_op jit(solution)/shard_map/cond/branch_4_fun/ppermute | solution.py:20
  111.0 1.6 multiply_add_fusion.38.refs_1_
  112.7 5.2 %collective-permute-start.37 = (f32[8,32768]{1,0:T(8,128)S(1)}, f32[8,32768]{1,0:T(8,128)}, u32[]{:S(2)}, u32[]{:S(2)}) collective-permute-start(f32[8,32768]{1,0:T(8,128)S(1)} %multiply_add_fusion.38.refs_1_), channel_id=1, source_target_pairs={{1,0},{2,1},{3,2},{4,3},{5,4},{6,5},{7,6},{8,7},{9,8},{10,9},{11,1... | collective-permute-start | bytes 3145736 | tf_op jit(solution)/shard_map/cond/branch_4_fun/ppermute | solution.py:20
  117.8 1.3 multiply_add_fusion.37.refs_2_
  119.8 2.3 %multiply_add_fusion.36.refs_3_ = f32[8,32768]{1,0:T(8,128)} fusion(f32[8,32768]{1,0:T(8,128)S(1)} %copy-done.9, f32[8,32768]{1,0:T(8,128)} %collective-permute-done.35), kind=kLoop, calls=%fused_computation.49 | loop fusion | flops 524288 | bytes 3145728 | tf_op jit(solution)/shard_map/cond/branch_4_fun/add | solution.py:120
  122.1 1.4 collective-permute-start.39
  123.5 1.0 multiply_subtract_fusion.4
  125.2 2.2 %all_gather.33.refs_4_ = f32[32,4096]{1,0:T(8,128)S(1)} all-gather(f32[32,2048]{1,0:T(8,128)S(1)} %multiply_subtract_fusion.4), channel_id=1, replica_groups=mesh['item'=2,'site'=16] {'item'}, dimensions={1}, use_global_device_ids=true | all-gather | bytes 786432 | tf_op jit(solution)/shard_map/cond/branch_4_fun/all_gather | solution.py:116
  127.4 18.8 %branch_4_fun.3 = (f32[8,32768]{1,0:T(8,128)S(1)}, f32[8,32768]{1,0:T(8,128)S(1)}, f32[8,32768]{1,0:T(8,128)S(1)}, f32[8,32768]{1,0:T(8,128)S(1)}, f32[32,4096]{1,0:T(8,128)S(1)}) custom-call(s32[128]{0:T(128)S(1)} %copy-done.112, s32[128]{0:T(128)S(1)} %copy-done.118, s32[1]{0:T(128)} %get-tuple-element.140.count_ref, ...), custom_call_target="tpu_custom_call" | custom-call | flops 1207959552 | bytes 12582912 | tf_op jit(solution)/shard_map/cond/branch_4_fun/pallas_call | solution.py:89
  146.2 1.0 copy-done.32
  147.2 1.0 copy-done.49
  149.2 1.0 copy-done.70
  151.0 1.8 multiply_add_fusion.35
  152.8 3.1 %collective-permute-done.37 = f32[8,32768]{1,0:T(8,128)} collective-permute-done((f32[8,32768]{1,0:T(8,128)S(1)}, f32[8,32768]{1,0:T(8,128)}, u32[]{:S(2)}, u32[]{:S(2)}) %collective-permute-start.37) | collective-permute-done | bytes 1048608 | tf_op jit(solution)/shard_map/cond/branch_4_fun/ppermute | solution.py:20
  156.0 1.6 multiply_add_fusion.34
  157.6 20.8 %collective-permute-done.38 = f32[8,32768]{1,0:T(8,128)} collective-permute-done((f32[8,32768]{1,0:T(8,128)S(1)}, f32[8,32768]{1,0:T(8,128)}, u32[]{:S(2)}, u32[]{:S(2)}) %collective-permute-start.38) | collective-permute-done | bytes 1048608 | tf_op jit(solution)/shard_map/cond/branch_4_fun/ppermute | solution.py:20
  178.4 1.3 multiply_add_fusion.33
  179.8 20.1 %collective-permute-done.39 = f32[8,32768]{1,0:T(8,128)} collective-permute-done((f32[8,32768]{1,0:T(8,128)}, f32[8,32768]{1,0:T(8,128)}, u32[]{:S(2)}, u32[]{:S(2)}) %collective-permute-start.39) | collective-permute-done | bytes 1048608 | tf_op jit(solution)/shard_map/cond/branch_4_fun/ppermute | solution.py:20
  199.9 1.3 multiply_add_fusion.32
  201.2 2.3 %maximum_bitcast_fusion.4 = f32[1,32,32768]{2,1,0:T(8,128)} fusion(f32[8,32768]{1,0:T(8,128)S(1)} %multiply_add_fusion.32, f32[8,32768]{1,0:T(8,128)S(1)} %multiply_add_fusion.33, f32[8,32768]{1,0:T(8,128)S(1)} %multiply_add_fusion.34, f32[8,32768]{1,0:T(8,128)S(1)} %multiply_add_fusion.35), kind=kLoop, calls=%fused_computation.44 | loop fusion | flops 3145728 | bytes 8388608 | tf_op jit(solution)/shard_map/broadcast_in_dim | solution.py:140
  203.5 1.7 subtract_bitcast_fusion.4
  (48 shorter events, 6.5 us)
Async XLA Ops:
  11.3 112.2 %reduce-scatter.29.cloned.1.call-start = ((), (), s32[]{:S(2)}) async-start(), calls=%async_computation.20 | async-start | bytes 786432 | tf_op jit(solution)/shard_map/cond/branch_4_fun/reduce_scatter | solution.py:121
  11.4 9.6 %copy-start.94 = (f32[32,2048]{1,0:T(8,128)S(1)}, f32[32,2048]{1,0:T(8,128)}, u32[]{:S(2)}) copy-start(f32[32,2048]{1,0:T(8,128)} %get-tuple-element.142) | copy-start | bytes 786436 | tf_op jit(solution)/shard_map/cond
  11.4 11.8 %copy-start.88 = (bf16[128,128,128]{2,1,0:T(8,128)(2,1)S(1)}, bf16[128,128,128]{2,1,0:T(8,128)(2,1)}, u32[]{:S(2)}) copy-start(bf16[128,128,128]{2,1,0:T(8,128)(2,1)} %get-tuple-element.143.refs_5_) | copy-start | bytes 12582916 | tf_op jit(solution)/shard_map/cond
  11.4 11.8 %copy-start.112 = (s32[128]{0:T(128)S(1)}, s32[128]{0:T(128)}, u32[]{:S(2)}) copy-start(s32[128]{0:T(128)} %get-tuple-element.138.rows_ref) | copy-start | bytes 1540 | tf_op jit(solution)/shard_map/cond
  11.4 11.8 %copy-start.118 = (s32[128]{0:T(128)S(1)}, s32[128]{0:T(128)}, u32[]{:S(2)}) copy-start(s32[128]{0:T(128)} %get-tuple-element.139.cols_ref) | copy-start | bytes 1540 | tf_op jit(solution)/shard_map/cond
  15.0 28.6 %collective-permute-start.32 = (f32[8,32768]{1,0:T(8,128)S(1)}, f32[8,32768]{1,0:T(8,128)}, u32[]{:S(2)}, u32[]{:S(2)}) collective-permute-start(f32[8,32768]{1,0:T(8,128)S(1)} %get-tuple-element.193.refs_0_), channel_id=1, source_target_pairs={{4,0},{5,1},{6,2},{7,3},{8,4},{9,5},{10,6},{11,7},{12,8},{13,9},{1... | collective-permute-start | bytes 3145736 | tf_op jit(solution)/shard_map/cond/branch_4_fun/ppermute | solution.py:20
  20.0 99.7 %collective-permute-start.35 = (f32[8,32768]{1,0:T(8,128)}, f32[8,32768]{1,0:T(8,128)}, u32[]{:S(2)}, u32[]{:S(2)}) collective-permute-start(f32[8,32768]{1,0:T(8,128)} %get-tuple-element.190.refs_3_), channel_id=1, source_target_pairs={{4,0},{5,1},{6,2},{7,3},{8,4},{9,5},{10,6},{11,7},{12,8},{13,9},{1... | collective-permute-start | bytes 3145736 | tf_op jit(solution)/shard_map/cond/branch_4_fun/ppermute | solution.py:20
  20.5 97.4 %collective-permute-start.34 = (f32[8,32768]{1,0:T(8,128)S(1)}, f32[8,32768]{1,0:T(8,128)}, u32[]{:S(2)}, u32[]{:S(2)}) collective-permute-start(f32[8,32768]{1,0:T(8,128)S(1)} %get-tuple-element.191.refs_2_), channel_id=1, source_target_pairs={{4,0},{5,1},{6,2},{7,3},{8,4},{9,5},{10,6},{11,7},{12,8},{13,9},{1... | collective-permute-start | bytes 3145736 | tf_op jit(solution)/shard_map/cond/branch_4_fun/ppermute | solution.py:20
  20.9 90.1 %collective-permute-start.33 = (f32[8,32768]{1,0:T(8,128)S(1)}, f32[8,32768]{1,0:T(8,128)}, u32[]{:S(2)}, u32[]{:S(2)}) collective-permute-start(f32[8,32768]{1,0:T(8,128)S(1)} %get-tuple-element.192.refs_1_), channel_id=1, source_target_pairs={{4,0},{5,1},{6,2},{7,3},{8,4},{9,5},{10,6},{11,7},{12,8},{13,9},{1... | collective-permute-start | bytes 3145736 | tf_op jit(solution)/shard_map/cond/branch_4_fun/ppermute | solution.py:20
  38.1 1.0 copy-start.8
  39.1 1.0 copy-start.20
  40.2 1.0 copy-start.48
  41.1 1.0 copy-start.64
  42.1 0.8 copy-start.76
  42.9 160.6 %reduce-scatter.31.cloned.1.call-start = ((), (), s32[]{:S(2)}) async-start(), calls=%async_computation.21 | async-start | bytes 786432 | tf_op jit(solution)/shard_map/cond/branch_4_fun/reduce_scatter | solution.py:121
  43.0 74.9 %copy-start.21 = (f32[8,32768]{1,0:T(8,128)S(1)}, f32[8,32768]{1,0:T(8,128)}, u32[]{:S(2)}) copy-start(f32[8,32768]{1,0:T(8,128)} %copy-done.20) | copy-start | bytes 3145732 | tf_op jit(solution)/shard_map/cond
  43.6 76.2 %copy-start.9 = (f32[8,32768]{1,0:T(8,128)S(1)}, f32[8,32768]{1,0:T(8,128)}, u32[]{:S(2)}) copy-start(f32[8,32768]{1,0:T(8,128)} %copy-done.8) | copy-start | bytes 3145732 | tf_op jit(solution)/shard_map/cond
  45.3 105.7 %collective-permute-start.36 = (f32[8,32768]{1,0:T(8,128)S(1)}, f32[8,32768]{1,0:T(8,128)}, u32[]{:S(2)}, u32[]{:S(2)}) collective-permute-start(f32[8,32768]{1,0:T(8,128)S(1)} %multiply_add_fusion.39.refs_0_), channel_id=1, source_target_pairs={{1,0},{2,1},{3,2},{4,3},{5,4},{6,5},{7,6},{8,7},{9,8},{10,9},{11,1... | collective-permute-start | bytes 3145736 | tf_op jit(solution)/shard_map/cond/branch_4_fun/ppermute | solution.py:20
  112.7 43.3 %collective-permute-start.37 = (f32[8,32768]{1,0:T(8,128)S(1)}, f32[8,32768]{1,0:T(8,128)}, u32[]{:S(2)}, u32[]{:S(2)}) collective-permute-start(f32[8,32768]{1,0:T(8,128)S(1)} %multiply_add_fusion.38.refs_1_), channel_id=1, source_target_pairs={{1,0},{2,1},{3,2},{4,3},{5,4},{6,5},{7,6},{8,7},{9,8},{10,9},{11,1... | collective-permute-start | bytes 3145736 | tf_op jit(solution)/shard_map/cond/branch_4_fun/ppermute | solution.py:20
  119.2 59.3 %collective-permute-start.38 = (f32[8,32768]{1,0:T(8,128)S(1)}, f32[8,32768]{1,0:T(8,128)}, u32[]{:S(2)}, u32[]{:S(2)}) collective-permute-start(f32[8,32768]{1,0:T(8,128)S(1)} %multiply_add_fusion.37.refs_2_), channel_id=1, source_target_pairs={{1,0},{2,1},{3,2},{4,3},{5,4},{6,5},{7,6},{8,7},{9,8},{10,9},{11,1... | collective-permute-start | bytes 3145736 | tf_op jit(solution)/shard_map/cond/branch_4_fun/ppermute | solution.py:20
  122.1 77.8 %collective-permute-start.39 = (f32[8,32768]{1,0:T(8,128)}, f32[8,32768]{1,0:T(8,128)}, u32[]{:S(2)}, u32[]{:S(2)}) collective-permute-start(f32[8,32768]{1,0:T(8,128)} %multiply_add_fusion.36.refs_3_), channel_id=1, source_target_pairs={{1,0},{2,1},{3,2},{4,3},{5,4},{6,5},{7,6},{8,7},{9,8},{10,9},{11,1... | collective-permute-start | bytes 3145736 | tf_op jit(solution)/shard_map/cond/branch_4_fun/ppermute | solution.py:20
  124.5 0.7 copy-start.104
  146.2 1.0 copy-start.32
  147.2 1.0 copy-start.49
  148.2 1.0 copy-start.58
  149.2 1.0 copy-start.70
  150.2 0.8 copy-start.82
  151.0 27.4 %copy-start.50 = (f32[8,32768]{1,0:T(8,128)S(1)}, f32[8,32768]{1,0:T(8,128)}, u32[]{:S(2)}) copy-start(f32[8,32768]{1,0:T(8,128)} %copy-done.49) | copy-start | bytes 3145732 | tf_op jit(solution)/shard_map/cond
  151.0 48.9 %copy-start.33 = (f32[8,32768]{1,0:T(8,128)S(1)}, f32[8,32768]{1,0:T(8,128)}, u32[]{:S(2)}) copy-start(f32[8,32768]{1,0:T(8,128)} %copy-done.32) | copy-start | bytes 3145732 | tf_op jit(solution)/shard_map/cond
  201.2 2.3 %copy-start.105 = (f32[32,2048]{1,0:T(8,128)S(1)}, f32[32,2048]{1,0:T(8,128)}, u32[]{:S(2)}) copy-start(f32[32,2048]{1,0:T(8,128)} %copy-done.104) | copy-start | bytes 786436 | tf_op jit(solution)/shard_map/cond
Sparse Core Ops, SparseCore 0:
  43.0 21.4 reduce-scatter.28
  151.1 13.5 reduce-scatter.30
where the time goes:
time: 213 us; the launch traced here: 212 us
  waiting for transfers between devices  104 us (49%)
  Pallas kernels  33.8 us (16%)
  starting transfers between devices  19.6 us (9%)
  other arithmetic  18 us (8%)
  between operations  16.6 us (8%)
  local copies, waits for them, and re-layouts  15.1 us (7%)
  blocking collectives  4.34 us (2%)
    ppermute x8, waiting for transfers between devices, passed_along(): return lax.ppermute(block, axis, route)  104 us
    pallas_call x2, Pallas kernels, local_grads(): pl.pallas_call(partial(grads_kernel, chunks), grid_spec=pltpu.PrefetchSca...  33.8 us
    ppermute x8, starting transfers between devices, passed_along(): return lax.ppermute(block, axis, route)  19.5 us
    add x8, other arithmetic, two_steps(): x_parts = [base + 0.5 * peer for base, peer in zip(bases, peers)]  13.1 us
    cond x40, local copies, waits for them, and re-layouts  10.2 us
    all_gather x2, blocking collectives, two_steps(): users_whole = lax.all_gather(user_here, 'item', axis=1, tiled=True)  4.34 us
  transfers between devices with their start and end apart: 10, of which 5 were waited for; matrix products, arithmetic and copies ran while one was open for 8% of the time, Pallas kernels for 16%

commit v1 on v0

--- a/solution.py
+++ b/solution.py
@@ -12,6 +12,7 @@
 LEARN_RATE = 0.05
 CHUNKS = 4
 GROUP = 8
+RELAYS = 4
 
 
 def passed_along(block, axis, distance):
@@ -123,13 +124,198 @@
     return jnp.concatenate(x_parts, axis=0), user_here
 
 
+def mix_kernel(hops, xs, bases, x1_first, x1s, q_lands, p_lands, hop_a, hop_b, *sems):
+    p_send, p_recv, q_send, q_recv, r_a, r_b, f_a, f_b = sems
+    site, item = lax.axis_index("site"), lax.axis_index("item")
+    sites = lax.axis_size("site")
+    place = lax.rem(site, RELAYS)
+    layer = site - place
+    ahead = lax.rem(site + sites - RELAYS, sites)
+    behind = lax.rem(site + RELAYS, sites)
+    width = x1_first.shape[1] // 2
+    part = width // RELAYS
+    steps = 2 * len(xs)
+
+    def view(ref, j):
+        return ref.at[:, pl.ds((j % 2) * width, width)]
+
+    def slab(ref, j, q):
+        return ref.at[:, pl.ds((j % 2) * width + q * part, part)]
+
+    def copy(src, dst, send, recv, target):
+        return pltpu.make_async_remote_copy(
+            src_ref=src,
+            dst_ref=dst,
+            send_sem=send,
+            recv_sem=recv,
+            device_id=(item, target),
+            device_id_type=pl.DeviceIdType.MESH,
+        )
+
+    barrier = pltpu.get_barrier_semaphore()
+    peers = [layer + lax.rem(place + k, RELAYS) for k in range(1, RELAYS)] + [ahead, behind]
+    for peer in peers:
+        pl.semaphore_signal(
+            barrier, inc=1, device_id=(item, peer), device_id_type=pl.DeviceIdType.MESH
+        )
+    pl.semaphore_wait(barrier, len(peers))
+
+    q_sources = [x1_first] + list(x1s[:-1])
+
+    def whole(flow, j):
+        src, land, send, recv = (
+            (xs[j // 2], p_lands[j // 2], p_send, p_recv)
+            if flow == 0
+            else (q_sources[j // 2], q_lands[j // 2], q_send, q_recv)
+        )
+        return src, land, send.at[j], recv.at[j]
+
+    def send(flow, j):
+        src, land, send_sem, recv_sem = whole(flow, j)
+        if hops[flow] != 0:
+            copy(view(src, j), view(land, j), send_sem, recv_sem, ahead).start()
+            return
+
+        @pl.when(place != 0)
+        def _():
+            copy(view(src, j), view(land, j), send_sem, recv_sem, site - 1).start()
+
+        @pl.when(place == 0)
+        def _():
+            copy(slab(src, j, 0), hop_b.at[j], send_sem, r_b.at[j], ahead).start()
+            for q in range(1, RELAYS):
+                copy(slab(src, j, q), hop_a.at[j], send_sem, r_a.at[j], site + q).start()
+
+    def relay(flow, j):
+        if hops[flow] != 0:
+            return
+        _, land, _, recv_sem = whole(flow, j)
+        last = RELAYS - 1
+
+        @pl.when(place != 0)
+        def _():
+            copy(hop_a.at[j], hop_a.at[j], f_a.at[j], r_a.at[j], ahead).wait_recv()
+
+        @pl.when(jnp.logical_and(place != 0, place != last))
+        def _():
+            copy(hop_a.at[j], hop_b.at[j], f_a.at[j], r_b.at[j], ahead).start()
+
+        @pl.when(place == last)
+        def _():
+            copy(hop_a.at[j], slab(land, j, last), f_a.at[j], recv_sem, ahead).start()
+
+        for q in range(last):
+
+            @pl.when(place == q)
+            def _():
+                copy(hop_b.at[j], hop_b.at[j], f_b.at[j], r_b.at[j], ahead).wait_recv()
+                copy(
+                    hop_b.at[j], slab(land, j, q), f_b.at[j], recv_sem, layer + last
+                ).start()
+
+    def relayed(flow, j):
+        if hops[flow] != 0:
+            return
+
+        @pl.when(place != 0)
+        def _():
+            copy(hop_a.at[j], hop_a.at[j], f_a.at[j], r_a.at[j], ahead).wait_send()
+
+        @pl.when(place != RELAYS - 1)
+        def _():
+            copy(hop_b.at[j], hop_b.at[j], f_b.at[j], r_b.at[j], ahead).wait_send()
+
+    def waiter(flow, j):
+        src, land, send_sem, recv_sem = whole(flow, j)
+        return copy(view(src, j), view(land, j), send_sem, recv_sem, ahead)
+
+    send(0, 0)
+    send(1, 0)
+    for j in range(steps):
+        if j + 1 < steps:
+            if j >= 1:
+                waiter(0, j - 1).wait_send()
+            send(0, j + 1)
+        relay(0, j)
+        waiter(0, j).wait_recv()
+        cols = pl.ds((j % 2) * width, width)
+        c = j // 2
+        x1s[c][:, cols] = bases[c][:, cols] + 0.5 * p_lands[c][:, cols]
+        if j + 1 < steps:
+            if j >= 1:
+                waiter(1, j - 1).wait_send()
+            send(1, j + 1)
+        relay(1, j)
+    waiter(0, steps - 2).wait_send()
+    waiter(0, steps - 1).wait_send()
+    waiter(1, steps - 2).wait_send()
+    waiter(1, steps - 1).wait_send()
+    for j in range(steps):
+        relayed(0, j)
+        relayed(1, j)
+        waiter(1, j).wait_recv()
+
+
+def mix(hops, xs, bases, x1_first):
+    n = len(xs)
+    rows, items = x1_first.shape
+    steps = 2 * n
+
+    def body(*refs):
+        refs = list(refs)
+        take = lambda k: [refs.pop(0) for _ in range(k)]
+        x, base = take(n), take(n)
+        (first,) = take(1)
+        x1, q_land, p_land = take(n), take(n), take(n)
+        mix_kernel(hops, x, base, first, x1, q_land, p_land, *refs)
+
+    whole_spec = pl.BlockSpec(memory_space=pltpu.VMEM)
+    chunk = jax.ShapeDtypeStruct((rows, items), jnp.float32)
+    relay_shape = pltpu.VMEM((steps, rows, items // (2 * RELAYS)), jnp.float32)
+    outs = pl.pallas_call(
+        body,
+        out_shape=[chunk] * (2 * n),
+        in_specs=[whole_spec] * (2 * n + 1),
+        out_specs=[whole_spec] * (2 * n),
+        scratch_shapes=[pltpu.VMEM((rows, items), jnp.float32)] * n
+        + [relay_shape, relay_shape]
+        + [pltpu.SemaphoreType.DMA((steps,))] * 8,
+        compiler_params=pltpu.CompilerParams(
+            collective_id=1 + hops[0], has_side_effects=True, vmem_limit_bytes=32 << 20
+        ),
+    )(*xs, *bases, x1_first)
+    return outs[:n], outs[n:]
+
+
+def two_steps_mixed(hops, item_here, user_here, slot_values, row_index, column_index, block_total):
+    rank = item_here.shape[0]
+    size = rank // CHUNKS
+    grads = lambda parts, users: local_grads(
+        parts, users, slot_values, row_index, column_index, block_total
+    )
+    x_parts = [item_here[c * size : (c + 1) * size] for c in range(CHUNKS)]
+    peer_first = passed_along(x_parts[0], "site", -(1 << hops[0]))
+    users_whole = lax.all_gather(user_here, "item", axis=1, tiled=True)
+    bases, user_grad = grads(x_parts, users_whole)
+    owned = lax.psum_scatter(user_grad, "item", scatter_dimension=1, tiled=True)
+    x1_first = bases[0] + 0.5 * peer_first
+    x1_rest, q_parts = mix(hops, x_parts[1:], bases[1:], x1_first)
+    peer_last = passed_along(x1_rest[-1], "site", -(1 << hops[1]))
+    user_here = user_here - LEARN_RATE * owned
+    users_whole = lax.all_gather(user_here, "item", axis=1, tiled=True)
+    bases, user_grad = grads([x1_first, *x1_rest], users_whole)
+    owned = lax.psum_scatter(user_grad, "item", scatter_dimension=1, tiled=True)
+    ends = [base + 0.5 * peer for base, peer in zip(bases, [*q_parts, peer_last])]
+    return jnp.concatenate(ends, axis=0), user_here - LEARN_RATE * owned
+
+
 def per_device(item_factors, user_factors, ratings, block_rows, block_cols, block_count, hop_steps):
     pairs = [(a, b) for a in range(HOPS) for b in range(HOPS) if a != b]
     first, second = hop_steps[0], hop_steps[1]
     chosen = first * (HOPS - 1) + second - (second > first).astype(jnp.int32)
     item_here, user_here = lax.switch(
         chosen,
-        [partial(two_steps, pair) for pair in pairs],
+        [partial(two_steps_mixed if 1 not in pair else two_steps, pair) for pair in pairs],
         item_factors[0],
         user_factors[0],
         ratings[0, 0],

time: 213 us -> 226 us (1.061); the launches traced: 212 us -> 230 us
  Pallas kernels: 33.8 us -> 122 us
  waiting for transfers between devices: 104 us -> 55.5 us
  starting transfers between devices: 19.6 us -> 7.84 us
  other arithmetic: 18 us -> 10.6 us
  local copies, waits for them, and re-layouts: 15.1 us -> 12.4 us
    pallas_call x0 -> x1, Pallas kernels: none -> 105 us  [mix(): pl.pallas_call(body, out_shape=[chunk] * (2 * n), in_specs=[whole_spec] *...]
    ppermute x8 -> x2, waiting for transfers between devices: 104 us -> 8.46 us  [passed_along(): return lax.ppermute(block, axis, route)]
    reduce_scatter x2, waiting for transfers between devices: 0.01 us -> 47 us  [two_steps_mixed(): owned = lax.psum_scatter(user_grad, 'item', scatter_dimension=1, tiled=True)]
    pallas_call x2, Pallas kernels: 33.8 us -> 16.8 us  [local_grads(): pl.pallas_call(partial(grads_kernel, chunks), grid_spec=pltpu.PrefetchSca...]
    ppermute x8 -> x2, starting transfers between devices: 19.5 us -> 7.76 us  [passed_along(): return lax.ppermute(block, axis, route)]
    add x8 -> x4, other arithmetic: 13.1 us -> 5.54 us  [the longest x3 3.9 us: two_steps_mixed(): base + 0.5 * peer]
    cond x40 -> x46, local copies, waits for them, and re-layouts: 10.2 us -> 8.46 us
  transfers between devices with their start and end apart: 10 -> 4, of which waited for: 5 -> 3; matrix products, arithmetic and copies ran while one was open for 8% -> 3% of each run, Pallas kernels for 16% -> 4%
where the time goes in v1:
time: 226 us; the launch traced here: 230 us
  Pallas kernels  122 us (54%)
  waiting for transfers between devices  55.5 us (25%)
  between operations  16.6 us (7%)
  local copies, waits for them, and re-layouts  12.4 us (5%)
  other arithmetic  10.6 us (5%)
  starting transfers between devices  7.84 us (3%)
  blocking collectives  4.65 us (2%)
    pallas_call x1, Pallas kernels, mix(): pl.pallas_call(body, out_shape=[chunk] * (2 * n), in_specs=[whole_spec] *...  105 us
    reduce_scatter x2, waiting for transfers between devices, two_steps_mixed(): owned = lax.psum_scatter(user_grad, 'item', scatter_dimension=1, tiled=True)  47 us
    pallas_call x2, Pallas kernels, local_grads(): pl.pallas_call(partial(grads_kernel, chunks), grid_spec=pltpu.PrefetchSca...  16.8 us
    cond x46, local copies, waits for them, and re-layouts  8.46 us
    ppermute x2, waiting for transfers between devices, passed_along(): return lax.ppermute(block, axis, route)  8.46 us
    ppermute x2, starting transfers between devices, passed_along(): return lax.ppermute(block, axis, route)  7.76 us
    all_gather x2, blocking collectives, two_steps_mixed(): users_whole = lax.all_gather(user_here, 'item', axis=1, tiled=True)  4.65 us
  transfers between devices with their start and end apart: 4, of which 3 were waited for; matrix products, arithmetic and copies ran while one was open for 3% of the time, Pallas kernels for 4%

profile of v1, /device:TPU:0, one launch (start us, length us, event | category | flops | bytes accessed | tf_op | source)
XLA Modules:
  0.0 230.1 jit_solution(12328500843945395823)
XLA Ops:
  7.2 1.3 fusion.6
  11.1 212.2 %conditional.1 = (f32[1,32,32768]{2,1,0:T(8,128)}, f32[1,32,2048]{2,1,0:T(8,128)}) conditional(s32[]{:T(128)} %clamp.3, (f32[32,32768]{1,0:T(8,128)}, f32[32,2048]{1,0:T(8,128)}, s32[128]{0:T(128)}, s32[128]{0:T(128)}, s32[1]{0:T(128)}, /*index=5*/bf16[128,128,128]{2,1,0:T(8,128)(2,1)}) %tuple.131, ...), branch_computations={%region_0.0_spmd, %region_3.0_spmd, %region_6.0_spmd, %region_9.0_... | conditional | flops 2423521280 | bytes 182981600 | solution.py:316
  11.1 0.0 reduce-scatter.17.cloned.1.call-start
  11.2 2.5 %all_gather.26.refs_4_ = f32[32,4096]{1,0:T(8,128)S(1)} all-gather(f32[32,2048]{1,0:T(8,128)} %get-tuple-element.94), channel_id=1, replica_groups=mesh['item'=2,'site'=16] {'item'}, dimensions={1}, use_global_device_ids=true | all-gather | bytes 786432 | tf_op jit(solution)/shard_map/cond/branch_1_fun/all_gather | solution.py:298
  13.6 2.6 %fusion.1 = (f32[8,32768]{1,0:T(8,128)S(1)}, f32[8,32768]{1,0:T(8,128)S(1)}, f32[8,32768]{1,0:T(8,128)S(1)}, f32[8,32768]{1,0:T(8,128)S(1)}) fusion(f32[32,32768]{1,0:T(8,128)} %get-tuple-element.93), kind=kLoop, calls=%fused_computation.61 | loop fusion | bytes 8388608 | tf_op jit(solution)/shard_map/cond/branch_1_fun/slice | solution.py:296
  16.3 0.8 copy-done.89
  17.1 7.8 %branch_1_fun.3 = (f32[8,32768]{1,0:T(8,128)S(1)}, f32[8,32768]{1,0:T(8,128)S(1)}, f32[8,32768]{1,0:T(8,128)S(1)}, f32[8,32768]{1,0:T(8,128)S(1)}, f32[32,4096]{1,0:T(8,128)S(1)}) custom-call(s32[128]{0:T(128)S(1)} %copy-done.115, s32[128]{0:T(128)S(1)} %copy-done.121, s32[1]{0:T(128)} %get-tuple-element.92.count_ref, ...), custom_call_target="tpu_custom_call" | custom-call | flops 1207959552 | bytes 12582912 | tf_op jit(solution)/shard_map/cond/branch_1_fun/pallas_call | solution.py:90
  24.9 1.0 copy-done.12
  25.9 1.0 copy-done.14
  26.9 1.0 copy-done.16
  27.9 1.0 copy-done.54
  28.9 0.8 copy-done.86
  29.7 0.0 reduce-scatter.19.cloned.1.call-start
  29.8 6.9 %collective-permute-start.8 = (f32[8,32768]{1,0:T(8,128)}, f32[8,32768]{1,0:T(8,128)}, u32[]{:S(2)}, u32[]{:S(2)}) collective-permute-start(f32[8,32768]{1,0:T(8,128)} %copy-done), channel_id=1, source_target_pairs={{1,0},{2,1},{3,2},{4,3},{5,4},{6,5},{7,6},{8,7},{9,8},{10,9},{11,1... | collective-permute-start | bytes 3145736 | tf_op jit(solution)/shard_map/cond/branch_1_fun/ppermute | solution.py:21
  36.7 20.9 %reduce-scatter.17.cloned.1.call-done = f32[32,2048]{1,0:T(8,128)} async-done(((f32[32,4096]{1,0:T(8,128)}), f32[32,2048]{1,0:T(8,128)}) %reduce-scatter.17.cloned.1.call-update) | async-done | bytes 262160 | tf_op jit(solution)/shard_map/cond/branch_1_fun/reduce_scatter | solution.py:300
  57.6 1.1 multiply_subtract_fusion.1
  58.7 2.2 all_gather.27.refs_4_
  60.9 1.6 multiply_add_fusion.12.refs_6_.refs_0_
  62.6 105.3 %branch_1_fun.4 = (f32[8,32768]{1,0:T(8,128)S(1)}, f32[8,32768]{1,0:T(8,128)S(1)}, f32[8,32768]{1,0:T(8,128)}, f32[8,32768]{1,0:T(8,128)S(1)}, f32[8,32768]{1,0:T(8,128)S(1)}, /*index=5*/f32[8,32768]{1,0:T(8,128)S(1)}) custom-call(f32[8,32768]{1,0:T(8,128)S(1)} %get-tuple-element.192.refs_1_.refs_0_, f32[8,32768]{1,0:T(8,128)S(1)} %get-tuple-element.191.refs_2_.refs_1_, ...), custom_call_target="tpu_custom_call" | custom-call | tf_op jit(solution)/shard_map/cond/branch_1_fun/pallas_call | solution.py:275
  167.9 0.9 collective-permute-start.9
  168.8 9.0 %branch_1_fun.5 = (f32[8,32768]{1,0:T(8,128)S(1)}, f32[8,32768]{1,0:T(8,128)S(1)}, f32[8,32768]{1,0:T(8,128)S(1)}, f32[8,32768]{1,0:T(8,128)S(1)}, f32[32,4096]{1,0:T(8,128)S(1)}) custom-call(s32[128]{0:T(128)S(1)} %copy-done.115, s32[128]{0:T(128)S(1)} %copy-done.121, s32[1]{0:T(128)} %get-tuple-element.92.count_ref, ...), custom_call_target="tpu_custom_call" | custom-call | flops 1207959552 | bytes 12582912 | tf_op jit(solution)/shard_map/cond/branch_1_fun/pallas_call | solution.py:90
  177.8 1.1 copy-done.72
  178.9 1.0 copy-done.73
  179.9 0.8 copy-done.84
  180.7 0.0 reduce-scatter.19.cloned.1.call-update
  180.7 2.5 %multiply_add_fusion.9 = (f32[8,32768]{1,0:T(8,128)S(1)}, f32[8,32768]{1,0:T(8,128)S(1)}) fusion(f32[8,32768]{1,0:T(8,128)} %copy-done.73, f32[8,32768]{1,0:T(8,128)} %copy-done.69, f32[8,32768]{1,0:T(8,128)} %copy-done.72, f32[8,32768]{1,0:T(8,128)} %copy-done.68), kind=kLoop, calls=%fused_computation.13 | loop fusion | flops 1048576 | bytes 6291456 | tf_op jit(solution)/shard_map/cond/branch_1_fun/add | solution.py:308
  183.2 0.1 multiply_add_fusion.11
  183.3 8.5 %collective-permute-done.9 = f32[8,32768]{1,0:T(8,128)} collective-permute-done((f32[8,32768]{1,0:T(8,128)}, f32[8,32768]{1,0:T(8,128)}, u32[]{:S(2)}, u32[]{:S(2)}) %collective-permute-start.9) | collective-permute-done | bytes 1048608 | tf_op jit(solution)/shard_map/cond/branch_1_fun/ppermute | solution.py:21
  191.7 1.3 multiply_add_fusion.8
  193.1 2.3 maximum_bitcast_fusion.1
  195.4 26.2 %reduce-scatter.19.cloned.1.call-done = f32[32,2048]{1,0:T(8,128)} async-done(((f32[32,4096]{1,0:T(8,128)}), f32[32,2048]{1,0:T(8,128)}) %reduce-scatter.19.cloned.1.call-update) | async-done | bytes 262160 | tf_op jit(solution)/shard_map/cond/branch_1_fun/reduce_scatter | solution.py:307
  221.6 1.7 subtract_bitcast_fusion.1
  (39 shorter events, 0.1 us)
Async XLA Ops:
  11.1 46.4 %reduce-scatter.17.cloned.1.call-start = ((), (), s32[]{:S(2)}) async-start(), calls=%async_computation.14 | async-start | bytes 786432 | tf_op jit(solution)/shard_map/cond/branch_1_fun/reduce_scatter | solution.py:300
  13.6 3.4 %copy-start.89 = (bf16[128,128,128]{2,1,0:T(8,128)(2,1)S(1)}, bf16[128,128,128]{2,1,0:T(8,128)(2,1)}, u32[]{:S(2)}) copy-start(bf16[128,128,128]{2,1,0:T(8,128)(2,1)} %get-tuple-element.95.refs_5_) | copy-start | bytes 12582916 | tf_op jit(solution)/shard_map/cond
  13.6 3.5 %copy-start.115 = (s32[128]{0:T(128)S(1)}, s32[128]{0:T(128)}, u32[]{:S(2)}) copy-start(s32[128]{0:T(128)} %get-tuple-element.90.rows_ref) | copy-start | bytes 1540 | tf_op jit(solution)/shard_map/cond
  13.6 3.5 %copy-start.121 = (s32[128]{0:T(128)S(1)}, s32[128]{0:T(128)}, u32[]{:S(2)}) copy-start(s32[128]{0:T(128)} %get-tuple-element.91.cols_ref) | copy-start | bytes 1540 | tf_op jit(solution)/shard_map/cond
  16.3 8.6 %copy-start = (f32[8,32768]{1,0:T(8,128)}, f32[8,32768]{1,0:T(8,128)S(1)}, u32[]{:S(2)}) copy-start(f32[8,32768]{1,0:T(8,128)S(1)} %get-tuple-element.193.refs_0_) | copy-start | bytes 3145732 | tf_op jit(solution)/shard_map/cond
  17.1 40.5 %copy-start.97 = (f32[32,2048]{1,0:T(8,128)S(1)}, f32[32,2048]{1,0:T(8,128)}, u32[]{:S(2)}) copy-start(f32[32,2048]{1,0:T(8,128)} %get-tuple-element.94) | copy-start | bytes 786436 | tf_op jit(solution)/shard_map/cond
  24.9 1.0 copy-start.12
  25.9 1.0 copy-start.14
  26.9 1.0 copy-start.16
  27.9 1.0 copy-start.54
  28.9 0.8 copy-start.86
  29.7 191.8 %reduce-scatter.19.cloned.1.call-start = ((), (), s32[]{:S(2)}) async-start(), calls=%async_computation.15 | async-start | bytes 786432 | tf_op jit(solution)/shard_map/cond/branch_1_fun/reduce_scatter | solution.py:307
  29.8 31.1 %collective-permute-start.8 = (f32[8,32768]{1,0:T(8,128)}, f32[8,32768]{1,0:T(8,128)}, u32[]{:S(2)}, u32[]{:S(2)}) collective-permute-start(f32[8,32768]{1,0:T(8,128)} %copy-done), channel_id=1, source_target_pairs={{1,0},{2,1},{3,2},{4,3},{5,4},{6,5},{7,6},{8,7},{9,8},{10,9},{11,1... | collective-permute-start | bytes 3145736 | tf_op jit(solution)/shard_map/cond/branch_1_fun/ppermute | solution.py:21
  57.5 5.0 %copy-start.13 = (f32[8,32768]{1,0:T(8,128)S(1)}, f32[8,32768]{1,0:T(8,128)}, u32[]{:S(2)}) copy-start(f32[8,32768]{1,0:T(8,128)} %copy-done.12) | copy-start | bytes 3145732 | tf_op jit(solution)/shard_map/cond
  57.5 5.0 %copy-start.15 = (f32[8,32768]{1,0:T(8,128)S(1)}, f32[8,32768]{1,0:T(8,128)}, u32[]{:S(2)}) copy-start(f32[8,32768]{1,0:T(8,128)} %copy-done.14) | copy-start | bytes 3145732 | tf_op jit(solution)/shard_map/cond
  57.5 5.0 %copy-start.17 = (f32[8,32768]{1,0:T(8,128)S(1)}, f32[8,32768]{1,0:T(8,128)}, u32[]{:S(2)}) copy-start(f32[8,32768]{1,0:T(8,128)} %copy-done.16) | copy-start | bytes 3145732 | tf_op jit(solution)/shard_map/cond
  58.7 2.2 copy-start.102
  62.5 106.2 %copy-start.90 = (bf16[128,128,128]{2,1,0:T(8,128)(2,1)S(1)}, bf16[128,128,128]{2,1,0:T(8,128)(2,1)}, u32[]{:S(2)}) copy-start(bf16[128,128,128]{2,1,0:T(8,128)(2,1)} %get-tuple-element.95.refs_5_) | copy-start | bytes 12582916 | tf_op jit(solution)/shard_map/cond
  167.9 9.9 %copy-start.32 = (f32[8,32768]{1,0:T(8,128)}, f32[8,32768]{1,0:T(8,128)S(1)}, u32[]{:S(2)}) copy-start(f32[8,32768]{1,0:T(8,128)S(1)} %get-tuple-element.105) | copy-start | bytes 3145732 | tf_op jit(solution)/shard_map/cond
  167.9 9.9 %copy-start.68 = (f32[8,32768]{1,0:T(8,128)}, f32[8,32768]{1,0:T(8,128)S(1)}, u32[]{:S(2)}) copy-start(f32[8,32768]{1,0:T(8,128)S(1)} %get-tuple-element.107) | copy-start | bytes 3145732 | tf_op jit(solution)/shard_map/cond
  167.9 9.9 %copy-start.69 = (f32[8,32768]{1,0:T(8,128)}, f32[8,32768]{1,0:T(8,128)S(1)}, u32[]{:S(2)}) copy-start(f32[8,32768]{1,0:T(8,128)S(1)} %get-tuple-element.109) | copy-start | bytes 3145732 | tf_op jit(solution)/shard_map/cond
  167.9 23.8 %collective-permute-start.9 = (f32[8,32768]{1,0:T(8,128)}, f32[8,32768]{1,0:T(8,128)}, u32[]{:S(2)}, u32[]{:S(2)}) collective-permute-start(f32[8,32768]{1,0:T(8,128)} %get-tuple-element.102.refs_3_), channel_id=1, source_target_pairs={{4,0},{5,1},{6,2},{7,3},{8,4},{9,5},{10,6},{11,7},{12,8},{13,9},{1... | collective-permute-start | bytes 3145736 | tf_op jit(solution)/shard_map/cond/branch_1_fun/ppermute | solution.py:21
  177.8 1.1 copy-start.72
  178.9 1.0 copy-start.73
  179.9 0.8 copy-start.84
  180.7 2.5 %copy-start.33 = (f32[8,32768]{1,0:T(8,128)S(1)}, f32[8,32768]{1,0:T(8,128)}, u32[]{:S(2)}) copy-start(f32[8,32768]{1,0:T(8,128)} %copy-done.32) | copy-start | bytes 3145732 | tf_op jit(solution)/shard_map/cond
  193.1 28.5 %copy-start.103 = (f32[32,2048]{1,0:T(8,128)S(1)}, f32[32,2048]{1,0:T(8,128)}, u32[]{:S(2)}) copy-start(f32[32,2048]{1,0:T(8,128)} %copy-done.102) | copy-start | bytes 786436 | tf_op jit(solution)/shard_map/cond
Sparse Core Ops, SparseCore 0:
  29.8 27.6 reduce-scatter.16
  180.8 40.6 reduce-scatter.18

commit v2 on v1

--- a/solution.py
+++ b/solution.py
@@ -13,6 +13,9 @@
 CHUNKS = 4
 GROUP = 8
 RELAYS = 4
+KERNEL_WEIGHT = 450
+MIX_WEIGHT = 100000
+BLEND_STEPS = 8
 
 
 def passed_along(block, axis, distance):
@@ -36,18 +39,18 @@
 def grads_kernel(chunks, rows_ref, cols_ref, count_ref, *refs):
     x_refs = refs[:chunks]
     y_ref, ratings_ref = refs[chunks : chunks + 2]
-    base_refs = refs[chunks + 2 : 2 * chunks + 2]
-    user_ref = refs[2 * chunks + 2]
+    base_ref, user_ref = refs[chunks + 2 :]
     group, tile = ratings_ref.shape[0], ratings_ref.shape[-1]
     rank = y_ref.shape[0]
-    part_rank = rank // chunks
     first = pl.program_id(0) * group
     total = count_ref[0]
 
     @pl.when(pl.program_id(0) == 0)
     def _():
-        for x_ref, base_ref in zip(x_refs, base_refs):
-            base_ref[...] = 0.5 * x_ref[...]
+        start = 0
+        for x_ref in x_refs:
+            base_ref[start : start + x_ref.shape[0], :] = 0.5 * x_ref[...]
+            start += x_ref.shape[0]
         user_ref[...] = jnp.zeros_like(user_ref)
 
     @pl.when(first < total)
@@ -74,8 +77,7 @@
             user_part = user_pair[:rank] + user_pair[rank:] + dot_f32(x_high, c_low, 1, 0)
             parts.append((row, col, item_part, user_part))
         for row, col, item_part, user_part in parts:
-            for c, base_ref in enumerate(base_refs):
-                base_ref[:, row] -= LEARN_RATE * item_part[c * part_rank : (c + 1) * part_rank]
+            base_ref[:, row] -= LEARN_RATE * item_part
             user_ref[:, col] += user_part
 
 
@@ -85,62 +87,115 @@
     rank, users = users_whole.shape
     items = x_parts[0].shape[1]
     once = pl.Buffered(1)
-    x_spec = pl.BlockSpec(x_parts[0].shape, lambda i, *_: (0, 0), pipeline_mode=once)
-    y_spec = pl.BlockSpec((rank, users), lambda i, *_: (0, 0), pipeline_mode=once)
-    outs = pl.pallas_call(
+    held = lambda shape: pl.BlockSpec(shape, lambda i, *_: (0, 0), pipeline_mode=once)
+    return pl.pallas_call(
         partial(grads_kernel, chunks),
         grid_spec=pltpu.PrefetchScalarGridSpec(
             num_scalar_prefetch=3,
             grid=(slot_total // GROUP,),
-            in_specs=[x_spec] * chunks
-            + [y_spec, pl.BlockSpec((GROUP, tile, tile), lambda i, *_: (i, 0, 0))],
-            out_specs=[x_spec] * chunks + [y_spec],
+            in_specs=[held(part.shape) for part in x_parts]
+            + [held((rank, users)), pl.BlockSpec((GROUP, tile, tile), lambda i, *_: (i, 0, 0))],
+            out_specs=[held((rank, items)), held((rank, users))],
         ),
-        out_shape=[jax.ShapeDtypeStruct(p.shape, jnp.float32) for p in x_parts]
-        + [jax.ShapeDtypeStruct((rank, users), jnp.float32)],
+        out_shape=[
+            jax.ShapeDtypeStruct((rank, items), jnp.float32),
+            jax.ShapeDtypeStruct((rank, users), jnp.float32),
+        ],
         compiler_params=pltpu.CompilerParams(vmem_limit_bytes=24 << 20),
         cost_estimate=pl.CostEstimate(
-            flops=18 * slot_total * tile * tile * rank,
+            flops=KERNEL_WEIGHT * slot_total * tile * tile * rank,
             bytes_accessed=8 * rank * items + 2 * slot_total * tile * tile,
             transcendentals=0,
         ),
     )(row_index, column_index, block_total, *x_parts, users_whole, slot_values)
-    return outs[:chunks], outs[chunks]
+
+
+def over_items(block):
+    total = block
+    for distance in range(1, lax.axis_size("item")):
+        total = total + passed_along(block, "item", distance)
+    return total
+
+
+def owned_part(whole):
+    count = lax.axis_size("item")
+    width = whole.shape[1] // count
+    me = lax.axis_index("item")
+    cut = lambda who: lax.dynamic_slice_in_dim(whole, who * width, width, axis=1)
+    total = cut(me)
+    for distance in range(1, count):
+        total = total + passed_along(cut(lax.rem(me + distance, count)), "item", distance)
+    return total
+
+
+def kept_part(whole):
+    width = whole.shape[1] // lax.axis_size("item")
+    return lax.dynamic_slice_in_dim(whole, lax.axis_index("item") * width, width, axis=1)
+
+
+def blend_kernel(base_ref, *refs):
+    out_ref = refs[-1]
+    start = 0
+    for ref in refs[:-1]:
+        rows = slice(start, start + ref.shape[0])
+        out_ref[rows, :] = base_ref[rows, :] + 0.5 * ref[...]
+        start += ref.shape[0]
+
+
+def blend(base, peers):
+    rank, items = base.shape
+    width = items // BLEND_STEPS
+    spec = lambda rows: pl.BlockSpec((rows, width), lambda i: (0, i))
+    return pl.pallas_call(
+        blend_kernel,
+        grid=(BLEND_STEPS,),
+        in_specs=[spec(rank)] + [spec(peer.shape[0]) for peer in peers],
+        out_specs=spec(rank),
+        out_shape=jax.ShapeDtypeStruct((rank, items), jnp.float32),
+    )(base, *peers)
+
+
+def cut_rows(block):
+    size = block.shape[0] // CHUNKS
+    return [block[c * size : (c + 1) * size] for c in range(CHUNKS)]
 
 
 def two_steps(hops, item_here, user_here, slot_values, row_index, column_index, block_total):
-    rank = item_here.shape[0]
-    size = rank // CHUNKS
-    x_parts = [item_here[c * size : (c + 1) * size] for c in range(CHUNKS)]
-    for hop in hops:
-        peers = [passed_along(part, "site", -(1 << hop)) for part in x_parts]
-        users_whole = lax.all_gather(user_here, "item", axis=1, tiled=True)
-        bases, user_grad = local_grads(
-            x_parts, users_whole, slot_values, row_index, column_index, block_total
-        )
-        x_parts = [base + 0.5 * peer for base, peer in zip(bases, peers)]
-        owned = lax.psum_scatter(user_grad, "item", scatter_dimension=1, tiled=True)
-        user_here = user_here - LEARN_RATE * owned
-    return jnp.concatenate(x_parts, axis=0), user_here
-
-
-def mix_kernel(hops, xs, bases, x1_first, x1s, q_lands, p_lands, hop_a, hop_b, *sems):
-    p_send, p_recv, q_send, q_recv, r_a, r_b, f_a, f_b = sems
+    grads = lambda parts, users: local_grads(
+        parts, users, slot_values, row_index, column_index, block_total
+    )
+    peers = [passed_along(part, "site", -(1 << hops[0])) for part in cut_rows(item_here)]
+    users_whole = lax.all_gather(user_here, "item", axis=1, tiled=True)
+    base, user_grad = grads([item_here], users_whole)
+    users_whole = users_whole - LEARN_RATE * over_items(user_grad)
+    x_parts = [part + 0.5 * peer for part, peer in zip(cut_rows(base), peers)]
+    peers = [passed_along(part, "site", -(1 << hops[1])) for part in x_parts]
+    base, user_grad = grads(x_parts, users_whole)
+    return blend(base, peers), kept_part(users_whole) - LEARN_RATE * owned_part(user_grad)
+
+
+def mix_kernel(hops, *refs):
+    x, base, x1_first, users, grad, x1_mid, x1_last, q_land, users_next = refs[:9]
+    p_land, grad_land, hop_a, hop_b, g_send, g_recv = refs[9:15]
+    p_send, p_recv, q_send, q_recv, r_a, r_b, f_a, f_b = refs[15:]
     site, item = lax.axis_index("site"), lax.axis_index("item")
     sites = lax.axis_size("site")
     place = lax.rem(site, RELAYS)
     layer = site - place
     ahead = lax.rem(site + sites - RELAYS, sites)
     behind = lax.rem(site + RELAYS, sites)
+    rows = x1_first.shape[0]
     width = x1_first.shape[1] // 2
     part = width // RELAYS
-    steps = 2 * len(xs)
-
-    def view(ref, j):
-        return ref.at[:, pl.ds((j % 2) * width, width)]
-
-    def slab(ref, j, q):
-        return ref.at[:, pl.ds((j % 2) * width + q * part, part)]
+    steps = 2 * q_land.shape[0] // rows
+
+    def view(at, j):
+        ref, start = at
+        return ref.at[pl.ds(start, rows), pl.ds((j % 2) * width, width)]
+
+    def slab(at, j, q):
+        ref, start = at
+        return ref.at[pl.ds(start, rows), pl.ds((j % 2) * width + q * part, part)]
 
     def copy(src, dst, send, recv, target):
         return pltpu.make_async_remote_copy(
@@ -158,17 +213,25 @@
         pl.semaphore_signal(
             barrier, inc=1, device_id=(item, peer), device_id_type=pl.DeviceIdType.MESH
         )
-    pl.semaphore_wait(barrier, len(peers))
-
-    q_sources = [x1_first] + list(x1s[:-1])
+    pl.semaphore_signal(
+        barrier, inc=1, device_id=(1 - item, site), device_id_type=pl.DeviceIdType.MESH
+    )
+    pl.semaphore_wait(barrier, len(peers) + 1)
+    swap = pltpu.make_async_remote_copy(
+        src_ref=grad,
+        dst_ref=grad_land,
+        send_sem=g_send,
+        recv_sem=g_recv,
+        device_id=(1 - item, site),
+        device_id_type=pl.DeviceIdType.MESH,
+    )
 
     def whole(flow, j):
-        src, land, send, recv = (
-            (xs[j // 2], p_lands[j // 2], p_send, p_recv)
-            if flow == 0
-            else (q_sources[j // 2], q_lands[j // 2], q_send, q_recv)
-        )
-        return src, land, send.at[j], recv.at[j]
+        start = (j // 2) * rows
+        if flow == 0:
+            return (x, start + rows), (p_land, start), p_send.at[j], p_recv.at[j]
+        src = (x1_first, 0) if j < 2 else (x1_mid, start - rows)
+        return src, (q_land, start), q_send.at[j], q_recv.at[j]
 
     def send(flow, j):
         src, land, send_sem, recv_sem = whole(flow, j)
@@ -231,6 +294,7 @@
 
     send(0, 0)
     send(1, 0)
+    swap.start()
     for j in range(steps):
         if j + 1 < steps:
             if j >= 1:
@@ -239,13 +303,18 @@
         relay(0, j)
         waiter(0, j).wait_recv()
         cols = pl.ds((j % 2) * width, width)
-        c = j // 2
-        x1s[c][:, cols] = bases[c][:, cols] + 0.5 * p_lands[c][:, cols]
+        start = (j // 2) * rows
+        out, at = (x1_last, 0) if j >= steps - 2 else (x1_mid, start)
+        out[at : at + rows, cols] = (
+            base[start + rows : start + 2 * rows, cols] + 0.5 * p_land[start : start + rows, cols]
+        )
         if j + 1 < steps:
             if j >= 1:
                 waiter(1, j - 1).wait_send()
             send(1, j + 1)
         relay(1, j)
+    swap.wait()
+    users_next[...] = users[...] - LEARN_RATE * (grad[...] + grad_land[...])
     waiter(0, steps - 2).wait_send()
     waiter(0, steps - 1).wait_send()
     waiter(1, steps - 2).wait_send()
@@ -256,66 +325,74 @@
         waiter(1, j).wait_recv()
 
 
-def mix(hops, xs, bases, x1_first):
-    n = len(xs)
+def mix(hops, x, base, x1_first, users, grad):
     rows, items = x1_first.shape
-    steps = 2 * n
-
-    def body(*refs):
-        refs = list(refs)
-        take = lambda k: [refs.pop(0) for _ in range(k)]
-        x, base = take(n), take(n)
-        (first,) = take(1)
-        x1, q_land, p_land = take(n), take(n), take(n)
-        mix_kernel(hops, x, base, first, x1, q_land, p_land, *refs)
-
+    rest = x.shape[0] - rows
+    steps = 2 * rest // rows
     whole_spec = pl.BlockSpec(memory_space=pltpu.VMEM)
-    chunk = jax.ShapeDtypeStruct((rows, items), jnp.float32)
+    shape = lambda n: jax.ShapeDtypeStruct((n, items), jnp.float32)
     relay_shape = pltpu.VMEM((steps, rows, items // (2 * RELAYS)), jnp.float32)
-    outs = pl.pallas_call(
-        body,
-        out_shape=[chunk] * (2 * n),
-        in_specs=[whole_spec] * (2 * n + 1),
-        out_specs=[whole_spec] * (2 * n),
-        scratch_shapes=[pltpu.VMEM((rows, items), jnp.float32)] * n
-        + [relay_shape, relay_shape]
+    return pl.pallas_call(
+        partial(mix_kernel, hops),
+        out_shape=[
+            shape(rest - rows),
+            shape(rows),
+            shape(rest),
+            jax.ShapeDtypeStruct(users.shape, jnp.float32),
+        ],
+        in_specs=[whole_spec] * 5,
+        out_specs=[whole_spec] * 4,
+        scratch_shapes=[
+            pltpu.VMEM((rest, items), jnp.float32),
+            pltpu.VMEM(users.shape, jnp.float32),
+            relay_shape,
+            relay_shape,
+            pltpu.SemaphoreType.DMA,
+            pltpu.SemaphoreType.DMA,
+        ]
         + [pltpu.SemaphoreType.DMA((steps,))] * 8,
         compiler_params=pltpu.CompilerParams(
             collective_id=1 + hops[0], has_side_effects=True, vmem_limit_bytes=32 << 20
         ),
-    )(*xs, *bases, x1_first)
-    return outs[:n], outs[n:]
+        cost_estimate=pl.CostEstimate(
+            flops=MIX_WEIGHT * rest * items,
+            bytes_accessed=16 * rest * items,
+            transcendentals=0,
+        ),
+    )(x, base, x1_first, users, grad)
 
 
 def two_steps_mixed(hops, item_here, user_here, slot_values, row_index, column_index, block_total):
-    rank = item_here.shape[0]
-    size = rank // CHUNKS
+    size = item_here.shape[0] // CHUNKS
     grads = lambda parts, users: local_grads(
         parts, users, slot_values, row_index, column_index, block_total
     )
-    x_parts = [item_here[c * size : (c + 1) * size] for c in range(CHUNKS)]
-    peer_first = passed_along(x_parts[0], "site", -(1 << hops[0]))
+    peer_first = passed_along(item_here[:size], "site", -(1 << hops[0]))
     users_whole = lax.all_gather(user_here, "item", axis=1, tiled=True)
-    bases, user_grad = grads(x_parts, users_whole)
-    owned = lax.psum_scatter(user_grad, "item", scatter_dimension=1, tiled=True)
-    x1_first = bases[0] + 0.5 * peer_first
-    x1_rest, q_parts = mix(hops, x_parts[1:], bases[1:], x1_first)
-    peer_last = passed_along(x1_rest[-1], "site", -(1 << hops[1]))
-    user_here = user_here - LEARN_RATE * owned
-    users_whole = lax.all_gather(user_here, "item", axis=1, tiled=True)
-    bases, user_grad = grads([x1_first, *x1_rest], users_whole)
-    owned = lax.psum_scatter(user_grad, "item", scatter_dimension=1, tiled=True)
-    ends = [base + 0.5 * peer for base, peer in zip(bases, [*q_parts, peer_last])]
-    return jnp.concatenate(ends, axis=0), user_here - LEARN_RATE * owned
+    base, user_grad = grads([item_here], users_whole)
+    x1_first = base[:size] + 0.5 * peer_first
+    x1_mid, x1_last, q_land, users_whole = mix(
+        hops, item_here, base, x1_first, users_whole, user_grad
+    )
+    peer_last = passed_along(x1_last, "site", -(1 << hops[1]))
+    base, user_grad = grads([x1_first, x1_mid, x1_last], users_whole)
+    users_out = kept_part(users_whole) - LEARN_RATE * owned_part(user_grad)
+    return blend(base, [q_land, peer_last]), users_out
 
 
 def per_device(item_factors, user_factors, ratings, block_rows, block_cols, block_count, hop_steps):
+    mixed = lambda pair: (
+        1 not in pair
+        and lax.axis_size("item") == 2
+        and lax.axis_size("site") % RELAYS == 0
+        and lax.axis_size("site") > 2 * RELAYS
+    )
     pairs = [(a, b) for a in range(HOPS) for b in range(HOPS) if a != b]
     first, second = hop_steps[0], hop_steps[1]
     chosen = first * (HOPS - 1) + second - (second > first).astype(jnp.int32)
     item_here, user_here = lax.switch(
         chosen,
-        [partial(two_steps_mixed if 1 not in pair else two_steps, pair) for pair in pairs],
+        [partial(two_steps_mixed if mixed(pair) else two_steps, pair) for pair in pairs],
         item_factors[0],
         user_factors[0],
         ratings[0, 0],

time: 226 us -> 187 us (0.83)
  the two profiles are of different devices: /device:TPU:0 before, /device:TPU:7 now
where the time goes in v2:
time: 187 us; the launch traced here: 185 us
  Pallas kernels  164 us (88%)
  local copies, waits for them, and re-layouts  8.9 us (5%)
  between operations  3.22 us (2%)
  blocking collectives  2.96 us (2%)
  starting transfers between devices  2.25 us (1%)
  other arithmetic  2.08 us (1%)
    pallas_call x1, Pallas kernels, mix(): pl.pallas_call(partial(mix_kernel, hops), out_shape=[shape(rest - rows),...  103 us
    pallas_call x2, Pallas kernels, local_grads(): pl.pallas_call(partial(grads_kernel, chunks), grid_spec=pltpu.PrefetchSca...  54 us
    pallas_call x1, Pallas kernels, blend(): pl.pallas_call(blend_kernel, grid=(BLEND_STEPS,), in_specs=[spec(rank)] +...  7.54 us
    cond x14, local copies, waits for them, and re-layouts  6.27 us
  transfers between devices with their start and end apart: 3, of which 1 were waited for; matrix products, arithmetic and copies ran while one was open for 0% of the time, Pallas kernels for 29%

profile of v2, /device:TPU:7, one launch (start us, length us, event | category | flops | bytes accessed | tf_op | source)
XLA Modules:
  0.0 185.3 jit_solution(11326442365783273347)
XLA Ops:
  0.6 1.3 fusion.4
  4.5 180.7 %conditional.1 = (f32[1,32,32768]{2,1,0:T(8,128)}, f32[1,32,2048]{2,1,0:T(8,128)}) conditional(s32[]{:T(128)} %clamp.3, (f32[32,2048]{1,0:T(8,128)}, s32[128]{0:T(128)}, s32[128]{0:T(128)}, s32[1]{0:T(128)}, f32[32,32768]{1,0:T(8,128)}, /*index=5*/bf16[128,128,128]{2,1,0:T(8,128)(2,1)}) %tuple.111, ...), branch_computations={%region_0.0_spmd, %region_1.0_spmd, %region_2.0_spmd, %region_3.0_... | conditional | flops 139041898496 | bytes 158602032 | solution.py:393
  4.6 1.3 slice.85
  5.9 0.3 collective-permute-start
  6.2 3.0 %all_gather.13.refs_1_.refs_3_ = f32[32,4096]{1,0:T(8,128)S(1)} all-gather(f32[32,2048]{1,0:T(8,128)} %get-tuple-element.88), channel_id=1, replica_groups=mesh['item'=2,'site'=16] {'item'}, dimensions={1}, use_global_device_ids=true | all-gather | bytes 786432 | tf_op jit(solution)/shard_map/cond/branch_1_fun/all_gather | solution.py:371
  9.1 28.2 %branch_1_fun.4 = (f32[32,32768]{1,0:T(8,128)S(1)}, f32[32,4096]{1,0:T(8,128)S(1)}) custom-call(s32[128]{0:T(128)} %get-tuple-element.84.rows_ref, s32[128]{0:T(128)} %get-tuple-element.85.cols_ref, s32[1]{0:T(128)} %get-tuple-element.86.count_ref, f32[32,32768]{1,0:T(8,128)} %get-tuple-element.87.refs_0_, f32[32,4096]{1,0:T(8,128)S(1)} %all_gather.13.refs_1_.refs_3_, ...), custom_call_target="tpu_custom_call" | custom-call | flops 30198988800 | bytes 12582912 | tf_op jit(solution)/shard_map/cond/branch_1_fun/pallas_call | solution.py:91
  37.4 0.0 copy-start.12
  37.4 2.0 %copy-done.12 = f32[32,32768]{1,0:T(8,128)} copy-done((f32[32,32768]{1,0:T(8,128)}, f32[32,32768]{1,0:T(8,128)S(1)}, u32[]{:S(2)}) %copy-start.12) | copy-done | bytes 4194328 | tf_op jit(solution)/shard_map/cond
  39.4 0.0 collective-permute-done
  39.4 1.3 multiply_add_fusion.4.refs_2_.refs_0_
  40.8 0.0 copy-start.13
  40.8 2.2 %copy-done.13 = f32[32,32768]{1,0:T(8,128)S(1)} copy-done((f32[32,32768]{1,0:T(8,128)S(1)}, f32[32,32768]{1,0:T(8,128)}, u32[]{:S(2)}) %copy-start.13) | copy-done | bytes 4194328 | tf_op jit(solution)/shard_map/cond
  42.9 0.0 copy-start.25
  43.0 0.0 copy-start.31
  43.0 0.0 copy-start.37
  43.0 102.6 %branch_1_fun.5 = (f32[16,32768]{1,0:T(8,128)S(1)}, f32[8,32768]{1,0:T(8,128)S(1)}, f32[24,32768]{1,0:T(8,128)S(1)}, f32[32,4096]{1,0:T(8,128)S(1)}) custom-call(f32[32,32768]{1,0:T(8,128)} %get-tuple-element.87.refs_0_, f32[32,32768]{1,0:T(8,128)S(1)} %copy-done.13, f32[8,32768]{1,0:T(8,128)S(1)} %multiply_add_fusion.4.refs_2_.refs_0_, ...), custom_call_target="tpu_custom_call" | custom-call | flops 78643200000 | bytes 12582912 | tf_op jit(solution)/shard_map/cond/branch_1_fun/pallas_call | solution.py:335
  145.6 0.0 copy-start.10
  145.6 1.9 %collective-permute-start.1 = (f32[8,32768]{1,0:T(8,128)S(1)}, f32[8,32768]{1,0:T(8,128)}, u32[]{:S(2)}, u32[]{:S(2)}) collective-permute-start(f32[8,32768]{1,0:T(8,128)S(1)} %get-tuple-element.93.refs_2_), channel_id=1, source_target_pairs={{4,0},{5,1},{6,2},{7,3},{8,4},{9,5},{10,6},{11,7},{12,8},{13,9},{1... | collective-permute-start | bytes 3145736 | tf_op jit(solution)/shard_map/cond/branch_1_fun/ppermute | solution.py:24
  147.5 0.0 copy-done.25
  147.5 0.0 copy-done.31
  147.5 0.0 copy-done.37
  147.5 25.8 %branch_1_fun.6 = (f32[32,32768]{1,0:T(8,128)S(1)}, f32[32,4096]{1,0:T(8,128)S(1)}) custom-call(s32[128]{0:T(128)S(1)} %copy-done.31, s32[128]{0:T(128)S(1)} %copy-done.37, s32[1]{0:T(128)} %get-tuple-element.86.count_ref, f32[8,32768]{1,0:T(8,128)S(1)} %multiply_add_fusion.4.refs_2_.refs_0_, f32[16,32768]{1,0:T(8,128)S(1)} %get-tuple-element.92.refs_1_, ...), custom_call_target="tpu_custom_call" | custom-call | flops 30198988800 | bytes 12582912 | tf_op jit(solution)/shard_map/cond/branch_1_fun/pallas_call | solution.py:91
  173.3 0.0 copy-done.10
  173.3 0.0 copy-start.8
  173.3 2.0 %copy-done.8 = f32[32,32768]{1,0:T(8,128)} copy-done((f32[32,32768]{1,0:T(8,128)}, f32[32,32768]{1,0:T(8,128)S(1)}, u32[]{:S(2)}) %copy-start.8) | copy-done | bytes 4194328 | tf_op jit(solution)/shard_map/cond
  175.4 0.1 collective-permute-start.2
  175.5 1.5 collective-permute-done.2
  177.0 0.7 subtract_bitcast_fusion.1
  177.7 0.0 collective-permute-done.1.refs_1_
  177.7 7.5 %branch_1_fun.7 = f32[32,32768]{1,0:T(8,128)} custom-call(f32[32,32768]{1,0:T(8,128)} %copy-done.8, f32[24,32768]{1,0:T(8,128)} %copy-done.10, f32[8,32768]{1,0:T(8,128)} %collective-permute-done.1.refs_1_), custom_call_target="tpu_custom_call" | custom-call | tf_op jit(solution)/shard_map/cond/branch_1_fun/pallas_call | solution.py:149
  (1 shorter events, 0.0 us)
Async XLA Ops:
  5.9 33.6 %collective-permute-start = (f32[8,32768]{1,0:T(8,128)S(1)}, f32[8,32768]{1,0:T(8,128)S(1)}, u32[]{:S(2)}, u32[]{:S(2)}) collective-permute-start(f32[8,32768]{1,0:T(8,128)S(1)} %slice.85), channel_id=1, source_target_pairs={{1,0},{2,1},{3,2},{4,3},{5,4},{6,5},{7,6},{8,7},{9,8},{10,9},{11,1... | collective-permute-start | bytes 3145736 | tf_op jit(solution)/shard_map/cond/branch_1_fun/ppermute | solution.py:24
  37.4 2.0 %copy-start.12 = (f32[32,32768]{1,0:T(8,128)}, f32[32,32768]{1,0:T(8,128)S(1)}, u32[]{:S(2)}) copy-start(f32[32,32768]{1,0:T(8,128)S(1)} %get-tuple-element.90.refs_1_) | copy-start | bytes 12582916 | tf_op jit(solution)/shard_map/cond
  40.8 2.2 %copy-start.13 = (f32[32,32768]{1,0:T(8,128)S(1)}, f32[32,32768]{1,0:T(8,128)}, u32[]{:S(2)}) copy-start(f32[32,32768]{1,0:T(8,128)} %copy-done.12) | copy-start | bytes 12582916 | tf_op jit(solution)/shard_map/cond
  42.9 104.5 %copy-start.25 = (bf16[128,128,128]{2,1,0:T(8,128)(2,1)S(1)}, bf16[128,128,128]{2,1,0:T(8,128)(2,1)}, u32[]{:S(2)}) copy-start(bf16[128,128,128]{2,1,0:T(8,128)(2,1)} %get-tuple-element.89.refs_2_.refs_4_) | copy-start | bytes 12582916 | tf_op jit(solution)/shard_map/cond
  43.0 104.5 %copy-start.31 = (s32[128]{0:T(128)S(1)}, s32[128]{0:T(128)}, u32[]{:S(2)}) copy-start(s32[128]{0:T(128)} %get-tuple-element.84.rows_ref) | copy-start | bytes 1540 | tf_op jit(solution)/shard_map/cond
  43.0 104.5 %copy-start.37 = (s32[128]{0:T(128)S(1)}, s32[128]{0:T(128)}, u32[]{:S(2)}) copy-start(s32[128]{0:T(128)} %get-tuple-element.85.cols_ref) | copy-start | bytes 1540 | tf_op jit(solution)/shard_map/cond
  145.6 27.7 %copy-start.10 = (f32[24,32768]{1,0:T(8,128)}, f32[24,32768]{1,0:T(8,128)S(1)}, u32[]{:S(2)}) copy-start(f32[24,32768]{1,0:T(8,128)S(1)} %get-tuple-element.96.refs_0_) | copy-start | bytes 9437188 | tf_op jit(solution)/shard_map/cond
  145.6 32.1 %collective-permute-start.1 = (f32[8,32768]{1,0:T(8,128)S(1)}, f32[8,32768]{1,0:T(8,128)}, u32[]{:S(2)}, u32[]{:S(2)}) collective-permute-start(f32[8,32768]{1,0:T(8,128)S(1)} %get-tuple-element.93.refs_2_), channel_id=1, source_target_pairs={{4,0},{5,1},{6,2},{7,3},{8,4},{9,5},{10,6},{11,7},{12,8},{13,9},{1... | collective-permute-start | bytes 3145736 | tf_op jit(solution)/shard_map/cond/branch_1_fun/ppermute | solution.py:24
  173.3 2.1 %copy-start.8 = (f32[32,32768]{1,0:T(8,128)}, f32[32,32768]{1,0:T(8,128)S(1)}, u32[]{:S(2)}) copy-start(f32[32,32768]{1,0:T(8,128)S(1)} %get-tuple-element.95.base_ref) | copy-start | bytes 12582916 | tf_op jit(solution)/shard_map/cond
  175.4 1.6 collective-permute-start.2
